TPU v7x, 32 devices: a whole 2x2x4 slice. The times are simulated.
32 devices in a mesh: row: 4 (over x, core), col: 8 (over z, y).
Axes of the slice: x: 2, y: 2, z: 4, core: 2. Of those that a mesh axis runs over, the one named last changes fastest.
Arguments:
- tokens: bfloat16 [1024, 2048], P('col'), may hold values from -6 to 6
- left_proj: bfloat16 [2048, 4096], P(None, 'row'), may hold values from -0.09375 to 0.09375
- teacher_up: bfloat16 [4096, 14848], P('row', 'col'), may hold values from -0.09375 to 0.09375
- right_proj: bfloat16 [14848, 7424], P('col', 'row'), may hold values from -0.046875 to 0.046875
- student_gate: bfloat16 [2048, 7424], P(None, 'row'), may hold values from -0.125 to 0.125
- target: bfloat16 [1024, 7424], P('col', 'row'), may hold values from -5 to 5
Outputs:
- grad_left: float32 [2048, 4096], P('col', 'row')
- grad_right: float32 [14848, 7424], P('col', 'row')
All inputs are finite; a program needn't handle non-finite values.
Results may differ from a plain program's by a relative error of at most 0.017.
Values may be sent and summed in bfloat16 or wider, within the bound.
A program may use at most 128 MiB of HBM per device.

v0:
```python
import math

import jax
import jax.numpy as jnp
from jax import lax
from jax.sharding import PartitionSpec as P


def up_gradient(gate_pre, up_pre, target, factor):
    gate_act = jax.nn.silu(gate_pre)
    return ((gate_act * up_pre - target.astype(jnp.float32)) * gate_act * factor).astype(
        jnp.bfloat16
    )


def shards(tokens, left_proj, teacher_up, right_proj, student_gate, target):
    col_count = lax.axis_size("col")
    factor = 1.0 / math.sqrt(tokens.shape[0] * col_count)
    picked = left_proj
    hidden_rows = lax.psum_scatter(
        jnp.dot(picked, teacher_up, preferred_element_type=jnp.float32),
        "row",
        scatter_dimension=0,
        tiled=True,
    ).astype(jnp.bfloat16)
    hidden_full = lax.all_gather(hidden_rows, "row", axis=0, tiled=True)
    picked = hidden_full
    up_rows = lax.psum_scatter(
        jnp.dot(picked, right_proj, preferred_element_type=jnp.float32),
        "col",
        scatter_dimension=0,
        tiled=True,
    ).astype(jnp.bfloat16)
    gate_pre = jnp.dot(tokens, student_gate, preferred_element_type=jnp.float32)
    contract_first = (((0,), (0,)), ((), ()))
    token_cols = lax.all_to_all(tokens, "col", split_axis=1, concat_axis=0, tiled=True)
    picked = token_cols
    up_pre = lax.psum_scatter(
        jnp.dot(picked, up_rows, preferred_element_type=jnp.float32),
        "col",
        scatter_dimension=0,
        tiled=True,
    )
    grad_up = up_gradient(gate_pre, up_pre, target, factor)
    grad_all = lax.all_gather(grad_up, "col", axis=0, tiled=True)
    grad_local = lax.dot_general(
        token_cols, grad_all, contract_first, preferred_element_type=jnp.float32
    ).astype(jnp.bfloat16)
    grad_student = lax.all_gather(grad_local, "col", axis=0, tiled=True)
    grad_right = lax.dot_general(
        hidden_full, grad_student, contract_first, preferred_element_type=jnp.float32
    )
    contract_second = (((1,), (1,)), ((), ()))
    picked = grad_student
    back_rows = lax.psum_scatter(
        lax.dot_general(
            picked, right_proj, contract_second, preferred_element_type=jnp.float32
        ).astype(jnp.bfloat16),
        "row",
        scatter_dimension=0,
        tiled=True,
    )
    back_full = lax.all_gather(back_rows, "row", axis=0, tiled=True)
    picked = back_full
    grad_left = lax.psum_scatter(
        lax.dot_general(picked, teacher_up, contract_second, preferred_element_type=jnp.float32),
        "col",
        scatter_dimension=0,
        tiled=True,
    )
    return (grad_left, grad_right)


def solution(mesh):
    return jax.shard_map(
        shards,
        mesh=mesh,
        in_specs=(
            P("col", None),
            P(None, "row"),
            P("row", "col"),
            P("col", "row"),
            P(None, "row"),
            P("col", "row"),
        ),
        out_specs=(P("col", "row"), P("col", "row")),
        check_vma=False,
    )
```

profile of v0, /device:TPU:0, one launch (start us, length us, event | category | flops | bytes accessed | tf_op | source)
XLA Modules:
  0.0 1122.3 jit_solution(11039336822752014126)
XLA Ops:
  7.2 14.1 %fusion.2 = f32[2048,1856]{0,1:T(8,128)} fusion(bf16[2048,1024]{1,0:T(8,128)(2,1)} %param.7, bf16[1024,1856]{0,1:T(8,128)(2,1)} %param.8), kind=kOutput, calls=%fused_computation.6 | convolution fusion | flops 7784628224 | bytes 23199744 | tf_op jit(solution)/shard_map/dot_general | solution.py:21
  21.4 116.1 %reduce-scatter.6.cloned.1.call-done = f32[512,1856]{0,1:T(8,128)} async-done(((f32[2048,1856]{0,1:T(8,128)}), f32[512,1856]{0,1:T(8,128)}) %reduce-scatter.6.cloned.1.call-update) | async-done | bytes 3801104 | tf_op jit(solution)/shard_map/reduce_scatter | solution.py:20
  137.6 3.6 convert_element_type.21
  141.2 53.9 %all-gather.5.cloned.1.call-done = bf16[2048,1856]{0,1:T(8,128)(2,1)} async-done(((bf16[512,1856]{0,1:T(8,128)(2,1)}), bf16[2048,1856]{0,1:T(8,128)(2,1)}) %all-gather.5.cloned.1.call-update) | async-done | bytes 7602192 | tf_op jit(solution)/shard_map/all_gather | solution.py:26
  195.1 22.1 %fusion.3 = f32[2048,1856]{0,1:T(8,128)} fusion(bf16[2048,1856]{0,1:T(8,128)(2,1)} %all-gather.5.cloned.1.call-done, bf16[1856,1856]{1,0:T(8,128)(2,1)} %param.9), kind=kOutput, calls=%fused_computation.7 | convolution fusion | flops 14109638656 | bytes 29696000 | tf_op jit(solution)/shard_map/dot_general | solution.py:29
  217.2 1.0 copy-done
  218.2 0.3 copy.8
  218.5 36.6 %all_to_all.19 = bf16[128,8,256]{0,2,1:T(8,128)(2,1)S(1)} all-to-all(bf16[128,8,256]{0,2,1:T(8,128)(2,1)S(1)} %bitcast.25), channel_id=1, replica_groups=mesh['row'=4,'col'=8] {'col'}, dimensions={1} | all-to-all | bytes 1048576 | tf_op jit(solution)/shard_map/all_to_all | solution.py:36
  255.1 0.2 copy.9
  255.3 221.3 %reduce-scatter.8.cloned.1.call-done = f32[256,1856]{0,1:T(8,128)} async-done(((f32[2048,1856]{0,1:T(8,128)}), f32[256,1856]{0,1:T(8,128)}) %reduce-scatter.8.cloned.1.call-update) | async-done | bytes 1900560 | tf_op jit(solution)/shard_map/reduce_scatter | solution.py:28
  476.6 5.9 convolution_bitcast_fusion
  482.5 0.2 all-gather.7.cloned.1.call-start
  482.7 136.0 %reduce-scatter.10.cloned.1.call-done = f32[128,1856]{0,1:T(8,128)} async-done(((f32[1024,1856]{0,1:T(8,128)}), f32[128,1856]{0,1:T(8,128)}) %reduce-scatter.10.cloned.1.call-update) | async-done | bytes 950288 | tf_op jit(solution)/shard_map/reduce_scatter | solution.py:38
  618.7 6.4 multiply_convert_fusion
  625.2 69.3 %all-gather.7.cloned.1.call-done = bf16[1024,1856]{0,1:T(8,128)(2,1)} async-done(((bf16[128,1856]{0,1:T(8,128)(2,1)}), bf16[1024,1856]{0,1:T(8,128)(2,1)}) %all-gather.7.cloned.1.call-update) | async-done | bytes 3801104 | tf_op jit(solution)/shard_map/all_gather | solution.py:45
  694.5 4.2 fusion
  698.7 113.6 %all-gather.9.cloned.1.call-done = bf16[2048,1856]{0,1:T(8,128)(2,1)} async-done(((bf16[256,1856]{0,1:T(8,128)(2,1)}), bf16[2048,1856]{0,1:T(8,128)(2,1)}) %all-gather.9.cloned.1.call-update) | async-done | bytes 7602192 | tf_op jit(solution)/shard_map/all_gather | solution.py:49
  812.3 21.3 %convolution_convert_fusion = bf16[2048,1856]{0,1:T(8,128)(2,1)} fusion(bf16[1856,1856]{1,0:T(8,128)(2,1)} %param.9, bf16[2048,1856]{0,1:T(8,128)(2,1)} %all-gather.9.cloned.1.call-done), kind=kOutput, calls=%fused_computation | convolution fusion | flops 14113439744 | bytes 22093824 | tf_op jit(solution)/shard_map/dot_general | solution.py:56
  833.8 64.6 %reduce-scatter.12.cloned.1.call-done = bf16[512,1856]{0,1:T(8,128)(2,1)} async-done(((bf16[2048,1856]{0,1:T(8,128)(2,1)}), bf16[512,1856]{0,1:T(8,128)(2,1)}) %reduce-scatter.12.cloned.1.call-update) | async-done | bytes 1900560 | tf_op jit(solution)/shard_map/reduce_scatter | solution.py:55
  898.4 0.3 reduce-scatter.14.cloned.1.call-start
  898.6 55.1 %all-gather.11.cloned.1.call-done = bf16[2048,1856]{0,1:T(8,128)(2,1)} async-done(((bf16[512,1856]{0,1:T(8,128)(2,1)}), bf16[2048,1856]{0,1:T(8,128)(2,1)}) %all-gather.11.cloned.1.call-update) | async-done | bytes 7602192 | tf_op jit(solution)/shard_map/all_gather | solution.py:63
  953.7 14.4 %fusion.4 = f32[2048,1024]{1,0:T(8,128)} fusion(bf16[2048,1856]{0,1:T(8,128)(2,1)} %all-gather.11.cloned.1.call-done, bf16[1024,1856]{0,1:T(8,128)(2,1)} %param.8), kind=kOutput, calls=%fused_computation.8 | convolution fusion | flops 7784628224 | bytes 19791872 | tf_op jit(solution)/shard_map/dot_general | solution.py:66
  968.2 22.1 %fusion.5 = f32[1856,1856]{1,0:T(8,128)} fusion(bf16[2048,1856]{0,1:T(8,128)(2,1)} %all-gather.5.cloned.1.call-done, bf16[2048,1856]{0,1:T(8,128)(2,1)} %all-gather.9.cloned.1.call-done), kind=kOutput, calls=%fused_computation.9 | convolution fusion | flops 14109638656 | bytes 28983296 | tf_op jit(solution)/shard_map/dot_general | solution.py:50
  990.3 125.5 %reduce-scatter.14.cloned.1.call-done = f32[256,1024]{1,0:T(8,128)} async-done(((f32[2048,1024]{1,0:T(8,128)}), f32[256,1024]{1,0:T(8,128)}) %reduce-scatter.14.cloned.1.call-update) | async-done | bytes 1048592 | tf_op jit(solution)/shard_map/reduce_scatter | solution.py:65
  (19 shorter events, 0.4 us)
Async XLA Ops:
  7.2 130.4 %reduce-scatter.6.cloned.1.call-start = ((), (), s32[]{:S(2)}) async-start(), calls=%async_computation.6 | async-start | bytes 19005440 | tf_op jit(solution)/shard_map/reduce_scatter | solution.py:20
  21.4 173.7 %all-gather.5.cloned.1.call-start = ((), (), s32[]{:S(2)}) async-start(), calls=%async_computation.7 | async-start | bytes 9502720 | tf_op jit(solution)/shard_map/all_gather | solution.py:26
  141.1 335.4 %reduce-scatter.8.cloned.1.call-start = ((), (), s32[]{:S(2)}) async-start(), calls=%async_computation.8 | async-start | bytes 17104896 | tf_op jit(solution)/shard_map/reduce_scatter | solution.py:28
  217.2 1.0 copy-start
  217.2 401.5 %reduce-scatter.10.cloned.1.call-start = ((), (), s32[]{:S(2)}) async-start(), calls=%async_computation.9 | async-start | bytes 8552448 | tf_op jit(solution)/shard_map/reduce_scatter | solution.py:38
  476.6 142.2 %copy-start.1 = (bf16[128,1856]{0,1:T(8,128)(2,1)S(1)}, bf16[128,1856]{0,1:T(8,128)(2,1)}, u32[]{:S(2)}) copy-start(bf16[128,1856]{0,1:T(8,128)(2,1)} %param.11) | copy-start | bytes 1425412
  482.5 212.0 %all-gather.7.cloned.1.call-start = ((), (), s32[]{:S(2)}) async-start(), calls=%async_computation.10 | async-start | bytes 4276224 | tf_op jit(solution)/shard_map/all_gather | solution.py:45
  625.1 187.2 %all-gather.9.cloned.1.call-start = ((), (), s32[]{:S(2)}) async-start(), calls=%async_computation.11 | async-start | bytes 8552448 | tf_op jit(solution)/shard_map/all_gather | solution.py:49
  698.7 199.7 %reduce-scatter.12.cloned.1.call-start = ((), (), s32[]{:S(2)}) async-start(), calls=%async_computation.12 | async-start | bytes 9502720 | tf_op jit(solution)/shard_map/reduce_scatter | solution.py:55
  833.7 120.0 %all-gather.11.cloned.1.call-start = ((), (), s32[]{:S(2)}) async-start(), calls=%async_computation.13 | async-start | bytes 9502720 | tf_op jit(solution)/shard_map/all_gather | solution.py:63
  898.4 217.4 %reduce-scatter.14.cloned.1.call-start = ((), (), s32[]{:S(2)}) async-start(), calls=%async_computation.14 | async-start | bytes 9437184 | tf_op jit(solution)/shard_map/reduce_scatter | solution.py:65
Sparse Core Ops, SparseCore 0:
  21.5 116.0 reduce-scatter.5
  141.3 53.7 all-gather.4
  217.3 259.2 reduce-scatter.7
  482.6 136.0 reduce-scatter.9
  625.2 69.1 all-gather.6
  698.8 113.5 all-gather.8
  833.8 64.4 reduce-scatter.11
  899.9 53.7 all-gather.10
  968.3 147.4 reduce-scatter.13
where the time goes:
time: 1120 us
  waiting for transfers between devices  956 us (85%)
  matrix products  110 us (10%)
  blocking collectives  36.6 us (3%)
  between operations  13.9 us (1%)
    reduce_scatter x1, waiting for transfers between devices, shards(): lax.psum_scatter(jnp.dot(picked, right_proj, preferred_element_type=jnp.f...  221 us
    reduce_scatter x1, waiting for transfers between devices, shards(): lax.psum_scatter(jnp.dot(picked, up_rows, preferred_element_type=jnp.floa...  136 us
    reduce_scatter x1, waiting for transfers between devices, shards(): lax.psum_scatter(lax.dot_general(picked, teacher_up, contract_second, pre...  126 us
    reduce_scatter x1, waiting for transfers between devices, shards(): lax.psum_scatter(jnp.dot(picked, teacher_up, preferred_element_type=jnp.f...  116 us
    all_gather x1, waiting for transfers between devices, shards(): grad_student = lax.all_gather(grad_local, 'col', axis=0, tiled=True)  114 us
    all_gather x1, waiting for transfers between devices, shards(): grad_all = lax.all_gather(grad_up, 'col', axis=0, tiled=True)  69.3 us
    reduce_scatter x1, waiting for transfers between devices, shards(): lax.psum_scatter(lax.dot_general(picked, right_proj, contract_second, pre...  64.6 us
    all_gather x1, waiting for transfers between devices, shards(): back_full = lax.all_gather(back_rows, 'row', axis=0, tiled=True)  55.1 us
  transfers between devices with their start and end apart: 9, of which 9 were waited for; matrix products, arithmetic and copies ran while one was open for 2% of the time, Pallas kernels for 0%

commit v1 on v0

v1 whole, which is shorter than its diff:
```python
import math

import jax
import jax.numpy as jnp
from jax import lax
from jax.sharding import PartitionSpec as P


def mm(a, b):
    return jnp.dot(a, b, preferred_element_type=jnp.float32)


def mm_nt(a, b):
    return lax.dot_general(a, b, (((1,), (1,)), ((), ())), preferred_element_type=jnp.float32)


def mm_tn(a, b):
    return lax.dot_general(a, b, (((0,), (0,)), ((), ())), preferred_element_type=jnp.float32)


def up_gradient(gate_pre, up_pre, target, factor):
    gate_act = jax.nn.silu(gate_pre)
    return ((gate_act * up_pre - target.astype(jnp.float32)) * gate_act * factor).astype(
        jnp.bfloat16
    )


def row_sum(partial):
    part = lax.psum_scatter(partial, "row", scatter_dimension=0, tiled=True)
    return lax.all_gather(part, "row", axis=0, tiled=True)


def shards(tokens, left_proj, teacher_up, right_proj, student_gate, target):
    bf16 = jnp.bfloat16
    factor = 1.0 / math.sqrt(tokens.shape[0] * lax.axis_size("col"))
    picked = lax.all_gather(mm(tokens, left_proj).astype(bf16), "col", axis=0, tiled=True)
    token_cols = lax.all_to_all(tokens, "col", split_axis=1, concat_axis=0, tiled=True)
    gate_pre = mm(tokens, student_gate)
    features = row_sum(mm(picked, teacher_up).astype(bf16))
    up_pre = lax.psum_scatter(
        mm(features, right_proj).astype(bf16), "col", scatter_dimension=0, tiled=True
    ).astype(jnp.float32)
    grad_up = up_gradient(gate_pre, up_pre, target, factor)
    grad_all = lax.all_gather(grad_up, "col", axis=0, tiled=True)
    back = row_sum(mm_nt(grad_all, right_proj).astype(bf16))
    grad_right = mm_tn(features, grad_all)
    units = lax.psum_scatter(
        mm_nt(back, teacher_up).astype(bf16), "col", scatter_dimension=0, tiled=True
    )
    units = lax.all_gather(units, "col", axis=0, tiled=True)
    grad_left = mm_tn(token_cols, units)
    return (grad_left, grad_right)


def solution(mesh):
    return jax.shard_map(
        shards,
        mesh=mesh,
        in_specs=(
            P("col", None),
            P(None, "row"),
            P("row", "col"),
            P("col", "row"),
            P(None, "row"),
            P("col", "row"),
        ),
        out_specs=(P("col", "row"), P("col", "row")),
        check_vma=False,
    )
```

time: 1120 us -> 557 us (0.50)
  waiting for transfers between devices: 956 us -> 438 us
  matrix products: 110 us -> 70 us
  blocking collectives: 36.6 us -> 24.6 us
    reduce_scatter x5 -> x3, waiting for transfers between devices: 664 us -> 149 us  [the longest x2 80.7 us: row_sum(): part = lax.psum_scatter(partial, 'row', scatter_dimension=0, tiled=True)]
    all_gather x3 -> x4, waiting for transfers between devices: 223 us -> 134 us  [the longest x2 68.5 us: row_sum(): return lax.all_gather(part, 'row', axis=0, tiled=True)]
    unnamed x9 -> x10, waiting for transfers between devices: 0.15 us -> 84.8 us
    dot_general x8, matrix products: 110 us -> 70 us  [the longest x4 32 us: mm(): return jnp.dot(a, b, preferred_element_type=jnp.float32)]
    all_to_all x1, blocking collectives: 36.6 us -> 24.6 us  [shards(): lax.all_to_all(tokens, 'col', split_axis=1, concat_axis=0, tiled=True)]
  transfers between devices with their start and end apart: 9 -> 9, of which waited for: 9 -> 9; matrix products, arithmetic and copies ran while one was open for 2% -> 3% of each run, Pallas kernels for 0% -> 0%
where the time goes in v1:
time: 557 us; the launch traced here: 556 us
  waiting for transfers between devices  438 us (79%)
  matrix products  70 us (13%)
  blocking collectives  24.6 us (4%)
  between operations  13.9 us (2%)
  local copies, waits for them, and re-layouts  9.23 us (2%)
    unnamed x10, waiting for transfers between devices  84.8 us
    reduce_scatter x2, waiting for transfers between devices, row_sum(): part = lax.psum_scatter(partial, 'row', scatter_dimension=0, tiled=True)  80.7 us
    all_gather x1, waiting for transfers between devices, shards(): grad_all = lax.all_gather(grad_up, 'col', axis=0, tiled=True)  69.7 us
    reduce_scatter x1, waiting for transfers between devices, shards(): lax.psum_scatter(mm_nt(back, teacher_up).astype(bf16), 'col', scatter_dim...  68.7 us
    all_gather x2, waiting for transfers between devices, row_sum(): return lax.all_gather(part, 'row', axis=0, tiled=True)  68.5 us
    all_gather x1, waiting for transfers between devices, shards(): lax.all_gather(mm(tokens, left_proj).astype(bf16), 'col', axis=0, tiled=T...  51.9 us
    dot_general x4, matrix products, mm(): return jnp.dot(a, b, preferred_element_type=jnp.float32)  32 us
    all_to_all x1, blocking collectives, shards(): lax.all_to_all(tokens, 'col', split_axis=1, concat_axis=0, tiled=True)  24.6 us
  transfers between devices with their start and end apart: 9, of which 9 were waited for; matrix products, arithmetic and copies ran while one was open for 3% of the time, Pallas kernels for 0%

profile of v1, /device:TPU:0, one launch (start us, length us, event | category | flops | bytes accessed | tf_op | source)
XLA Modules:
  0.0 556.5 jit_solution(13395948828155870849)
XLA Ops:
  7.2 3.8 convolution_convert_fusion.4
  11.1 51.9 %all-gather.6.cloned.1.call-done = bf16[1024,1024]{1,0:T(8,128)(2,1)} async-done(((bf16[128,1024]{1,0:T(8,128)(2,1)}), bf16[1024,1024]{1,0:T(8,128)(2,1)}) %all-gather.6.cloned.1.call-update) | async-done | bytes 2097168 | tf_op jit(solution)/shard_map/all_gather | solution.py:36
  63.0 8.7 %convolution_convert_fusion.2 = bf16[1024,1856]{0,1:T(8,128)(2,1)} fusion(bf16[1024,1024]{1,0:T(8,128)(2,1)} %all-gather.6.cloned.1.call-done, bf16[1024,1856]{0,1:T(8,128)(2,1)} %param.8), kind=kOutput, calls=%fused_computation.2 | convolution fusion | flops 3894214656 | bytes 9699328 | tf_op jit(solution)/shard_map/dot_general | solution.py:10
  71.8 40.5 %reduce-scatter.7.cloned.1.call-done = bf16[256,1856]{0,1:T(8,128)(2,1)} async-done(((bf16[1024,1856]{0,1:T(8,128)(2,1)}), bf16[256,1856]{0,1:T(8,128)(2,1)}) %reduce-scatter.7.cloned.1.call-update) | async-done | bytes 950288 | tf_op jit(solution)/shard_map/reduce_scatter | solution.py:29
  112.4 34.2 %all-gather.8.cloned.1.call-done = bf16[1024,1856]{0,1:T(8,128)(2,1)} async-done(((bf16[256,1856]{0,1:T(8,128)(2,1)}), bf16[1024,1856]{0,1:T(8,128)(2,1)}) %all-gather.8.cloned.1.call-update) | async-done | bytes 3801104 | tf_op jit(solution)/shard_map/all_gather | solution.py:30
  146.6 13.4 %convolution_convert_fusion.1 = bf16[1024,1856]{0,1:T(8,128)(2,1)} fusion(bf16[1024,1856]{0,1:T(8,128)(2,1)} %all-gather.8.cloned.1.call-done, bf16[1856,1856]{1,0:T(8,128)(2,1)} %param.9), kind=kOutput, calls=%fused_computation.1 | convolution fusion | flops 7056719872 | bytes 14491648 | tf_op jit(solution)/shard_map/dot_general | solution.py:10
  160.0 6.1 %copy.16 = bf16[1024,1856]{1,0:T(8,128)(2,1)} copy(bf16[1024,1856]{0,1:T(8,128)(2,1)} %convolution_convert_fusion.1) | data formatting | bytes 7602176
  166.2 84.6 %reduce-scatter.13.cloned.1.call-done = bf16[128,1856]{1,0:T(8,128)(2,1)} async-done(((bf16[1024,1856]{1,0:T(8,128)(2,1)}), bf16[128,1856]{1,0:T(8,128)(2,1)}) %reduce-scatter.13.cloned.1.call-update) | async-done | bytes 475152
  250.8 1.3 copy.17
  252.2 6.2 %multiply_convert_fusion = bf16[128,1856]{0,1:T(8,128)(2,1)} fusion(bf16[128,1856]{0,1:T(8,128)(2,1)S(1)} %copy-done.1, bf16[128,1856]{0,1:T(8,128)(2,1)S(1)} %copy.17, bf16[128,2048]{1,0:T(8,128)(2,1)S(1)} %copy-done, bf16[2048,1856]{0,1:T(8,128)(2,1)} %param.10), kind=kOutput, calls=%fused_computation.6 | convolution fusion | flops 975691776 | bytes 9551872 | tf_op jit(solution)/shard_map/dot_general | solution.py:10
  258.3 0.2 reduce-scatter.9.cloned.1.call-start
  258.6 69.7 %all-gather.10.cloned.1.call-done = bf16[1024,1856]{0,1:T(8,128)(2,1)} async-done(((bf16[128,1856]{0,1:T(8,128)(2,1)}), bf16[1024,1856]{0,1:T(8,128)(2,1)}) %all-gather.10.cloned.1.call-update) | async-done | bytes 3801104 | tf_op jit(solution)/shard_map/all_gather | solution.py:44
  328.3 12.6 %convolution_convert_fusion = bf16[1024,1856]{0,1:T(8,128)(2,1)} fusion(bf16[1856,1856]{1,0:T(8,128)(2,1)} %param.9, bf16[1024,1856]{0,1:T(8,128)(2,1)} %all-gather.10.cloned.1.call-done), kind=kOutput, calls=%fused_computation | convolution fusion | flops 7056719872 | bytes 14491648 | tf_op jit(solution)/shard_map/dot_general | solution.py:14
  340.9 40.2 %reduce-scatter.9.cloned.1.call-done = bf16[256,1856]{0,1:T(8,128)(2,1)} async-done(((bf16[1024,1856]{0,1:T(8,128)(2,1)}), bf16[256,1856]{0,1:T(8,128)(2,1)}) %reduce-scatter.9.cloned.1.call-update) | async-done | bytes 950288 | tf_op jit(solution)/shard_map/reduce_scatter | solution.py:29
  381.2 34.2 %all-gather.12.cloned.1.call-done = bf16[1024,1856]{0,1:T(8,128)(2,1)} async-done(((bf16[256,1856]{0,1:T(8,128)(2,1)}), bf16[1024,1856]{0,1:T(8,128)(2,1)}) %all-gather.12.cloned.1.call-update) | async-done | bytes 3801104 | tf_op jit(solution)/shard_map/all_gather | solution.py:30
  415.4 9.1 %convolution_convert_fusion.3 = bf16[1024,1024]{1,0:T(8,128)(2,1)} fusion(bf16[1024,1856]{0,1:T(8,128)(2,1)} %all-gather.12.cloned.1.call-done, bf16[1024,1856]{0,1:T(8,128)(2,1)} %param.8), kind=kOutput, calls=%fused_computation.3 | convolution fusion | flops 3893362688 | bytes 9699328 | tf_op jit(solution)/shard_map/dot_general | solution.py:14
  424.6 68.7 %reduce-scatter.11.cloned.1.call-done = bf16[128,1024]{1,0:T(8,128)(2,1)} async-done(((bf16[1024,1024]{1,0:T(8,128)(2,1)}), bf16[128,1024]{1,0:T(8,128)(2,1)}) %reduce-scatter.11.cloned.1.call-update) | async-done | bytes 262160 | tf_op jit(solution)/shard_map/reduce_scatter | solution.py:47
  493.4 0.3 copy.13
  493.6 24.6 %all_to_all.19 = bf16[128,8,256]{0,2,1:T(8,128)(2,1)S(1)} all-to-all(bf16[128,8,256]{0,2,1:T(8,128)(2,1)S(1)} %bitcast.23), channel_id=1, replica_groups=mesh['row'=4,'col'=8] {'col'}, dimensions={1} | all-to-all | bytes 1048576 | tf_op jit(solution)/shard_map/all_to_all | solution.py:37
  518.2 0.2 copy.14
  518.4 13.9 %fusion = f32[1856,1856]{1,0:T(8,128)} fusion(bf16[1024,1856]{0,1:T(8,128)(2,1)} %all-gather.8.cloned.1.call-done, bf16[1024,1856]{0,1:T(8,128)(2,1)} %all-gather.10.cloned.1.call-done), kind=kOutput, calls=%fused_computation.7 | convolution fusion | flops 7054819328 | bytes 21381120 | tf_op jit(solution)/shard_map/dot_general | solution.py:18
  532.3 14.0 %all-gather.14.cloned.1.call-done = bf16[1024,1024]{1,0:T(8,128)(2,1)} async-done(((bf16[128,1024]{1,0:T(8,128)(2,1)}), bf16[1024,1024]{1,0:T(8,128)(2,1)}) %all-gather.14.cloned.1.call-update) | async-done | bytes 2097168 | tf_op jit(solution)/shard_map/all_gather | solution.py:50
  546.3 2.3 convolution_bitcast_fusion
  548.6 1.3 copy.15
  (21 shorter events, 0.5 us)
Async XLA Ops:
  7.2 55.8 %all-gather.6.cloned.1.call-start = ((), (), s32[]{:S(2)}) async-start(), calls=%async_computation.5 | async-start | bytes 2359296 | tf_op jit(solution)/shard_map/all_gather | solution.py:36
  11.0 101.3 %reduce-scatter.7.cloned.1.call-start = ((), (), s32[]{:S(2)}) async-start(), calls=%async_computation.6 | async-start | bytes 4751360 | tf_op jit(solution)/shard_map/reduce_scatter | solution.py:29
  71.7 74.9 %all-gather.8.cloned.1.call-start = ((), (), s32[]{:S(2)}) async-start(), calls=%async_computation.7 | async-start | bytes 4751360 | tf_op jit(solution)/shard_map/all_gather | solution.py:30
  112.4 138.5 %reduce-scatter.13.cloned.1.call-start = ((), (), s32[]{:S(2)}) async-start(), calls=%async_computation.13 | async-start | bytes 4423680
  166.1 86.0 %copy-start = (bf16[128,2048]{1,0:T(8,128)(2,1)S(1)}, bf16[128,2048]{1,0:T(8,128)(2,1)}, u32[]{:S(2)}) copy-start(bf16[128,2048]{1,0:T(8,128)(2,1)} %param.6) | copy-start | bytes 1572868
  166.1 86.0 %copy-start.1 = (bf16[128,1856]{0,1:T(8,128)(2,1)S(1)}, bf16[128,1856]{0,1:T(8,128)(2,1)}, u32[]{:S(2)}) copy-start(bf16[128,1856]{0,1:T(8,128)(2,1)} %param.11) | copy-start | bytes 1425412
  166.2 162.1 %all-gather.10.cloned.1.call-start = ((), (), s32[]{:S(2)}) async-start(), calls=%async_computation.8 | async-start | bytes 4276224 | tf_op jit(solution)/shard_map/all_gather | solution.py:44
  258.3 122.8 %reduce-scatter.9.cloned.1.call-start = ((), (), s32[]{:S(2)}) async-start(), calls=%async_computation.9 | async-start | bytes 4751360 | tf_op jit(solution)/shard_map/reduce_scatter | solution.py:29
  340.9 74.5 %all-gather.12.cloned.1.call-start = ((), (), s32[]{:S(2)}) async-start(), calls=%async_computation.10 | async-start | bytes 4751360 | tf_op jit(solution)/shard_map/all_gather | solution.py:30
  381.1 112.2 %reduce-scatter.11.cloned.1.call-start = ((), (), s32[]{:S(2)}) async-start(), calls=%async_computation.11 | async-start | bytes 2359296 | tf_op jit(solution)/shard_map/reduce_scatter | solution.py:47
  424.6 121.7 %all-gather.14.cloned.1.call-start = ((), (), s32[]{:S(2)}) async-start(), calls=%async_computation.12 | async-start | bytes 2359296 | tf_op jit(solution)/shard_map/all_gather | solution.py:50
Sparse Core Ops, SparseCore 0:
  11.1 51.7 all-gather.5
  71.9 40.4 reduce-scatter.6
  113.9 32.7 all-gather.7
  166.3 84.5 reduce-scatter.12
  258.5 69.7 all-gather.9
  341.0 40.0 reduce-scatter.8
  382.7 32.7 all-gather.11
  424.7 68.5 reduce-scatter.10
  495.5 50.7 all-gather.13

commit v2 on v1

v2 whole, which is shorter than its diff:
```python
import functools
import math

import jax
import jax.numpy as jnp
from jax import lax
from jax.experimental import pallas as pl
from jax.experimental.pallas import tpu as pltpu
from jax.sharding import PartitionSpec as P

MESH = pl.DeviceIdType.MESH
BF16 = jnp.bfloat16
F32 = jnp.float32
STRIP = 16


def mm(a, b):
    return jnp.dot(a, b, preferred_element_type=F32)


def mm_nt(a, b):
    return lax.dot_general(a, b, (((1,), (1,)), ((), ())), preferred_element_type=F32)


def mm_tn(a, b):
    return lax.dot_general(a, b, (((0,), (0,)), ((), ())), preferred_element_type=F32)


def block(index, size):
    return pl.ds(pl.multiple_of(index * size, size), size)


def send(src, dst, send_sem, recv_sem, axis, peer):
    return pltpu.make_async_remote_copy(
        src_ref=src,
        dst_ref=dst,
        send_sem=send_sem,
        recv_sem=recv_sem,
        device_id={axis: peer},
        device_id_type=MESH,
    )


def meet(axis, peers):
    barrier = pltpu.get_barrier_semaphore()
    for peer in peers:
        pl.semaphore_signal(barrier, inc=1, device_id={axis: peer}, device_id_type=MESH)
    pl.semaphore_wait(barrier, len(peers))


def add_strips(out, out_at, terms, rows):
    @pl.loop(0, rows // STRIP)
    def _(t):
        total = None
        for ref, at in terms:
            part = ref[pl.ds(pl.multiple_of(at + t * STRIP, STRIP), STRIP), :].astype(F32)
            total = part if total is None else total + part
        out[pl.ds(pl.multiple_of(out_at + t * STRIP, STRIP), STRIP), :] = total.astype(out.dtype)


def split_of(count):
    inner = 1
    while inner * inner * 4 <= count and count % (inner * 2) == 0:
        inner *= 2
    return count // inner, inner


def place(count):
    outer, inner = split_of(count)
    me = lax.axis_index("col")
    hi, lo = lax.div(me, inner), lax.rem(me, inner)
    return outer, inner, me, hi, lo


def gather_body(count, x, out, send_hi, recv_hi, send_lo, recv_lo):
    outer, inner, me, hi, lo = place(count)
    rows = x.shape[0]

    def at(h, l):
        return block(h * inner + l, rows)

    def to_hi(d):
        return send(x, out.at[at(hi, lo)], send_hi.at[d - 1], recv_hi.at[d - 1], "col",
                    lax.rem(hi + d, outer) * inner + lo)

    def to_lo(d, e):
        h = lax.rem(hi + outer - d, outer)
        src = x if d == 0 else out.at[at(h, lo)]
        return send(src, out.at[at(h, lo)], send_lo.at[d, e - 1], recv_lo.at[d, e - 1], "col",
                    hi * inner + lax.rem(lo + e, inner))

    for e in range(1, inner):
        to_lo(0, e).start()
    for d in range(1, outer):
        to_hi(d).start()
    out[at(hi, lo), :] = x[...]
    for d in range(1, outer):
        to_hi(d).wait_recv()
        for e in range(1, inner):
            to_lo(d, e).start()
    for d in range(outer):
        for e in range(1, inner):
            to_lo(d, e).wait()
    for d in range(1, outer):
        to_hi(d).wait_send()


def line_peers(count):
    outer, inner, me, hi, lo = place(count)
    return [lax.rem(hi + d, outer) * inner + lo for d in range(1, outer)] + [
        hi * inner + lax.rem(lo + e, inner) for e in range(1, inner)
    ]


def gather_sems(count):
    outer, inner = split_of(count)
    dma = pltpu.SemaphoreType.DMA
    far, near = (outer - 1,), (outer, max(inner - 1, 1))
    return [dma(far), dma(far), dma(near), dma(near)]


def gather_kernel(count, x, out, *sems):
    meet("col", line_peers(count))
    gather_body(count, x, out, *sems)


def gather_turn_kernel(count, x, tokens, out, turned, turn_send, turn_recv, *sems):
    me = lax.axis_index("col")
    meet("col", [lax.rem(me + d, count) for d in range(1, count)])
    rows, width = tokens.shape[0], turned.shape[1]

    def turn(d):
        peer = lax.rem(me + d, count)
        return send(tokens.at[:, block(peer, width)], turned.at[block(me, rows)],
                    turn_send.at[d - 1], turn_recv.at[d - 1], "col", peer)

    gather_body(count, x, out, *sems)
    for d in range(1, count):
        turn(d).start()
    turned[block(me, rows), :] = tokens[:, block(me, width)]
    for d in range(1, count):
        turn(d).wait()


def scatter_kernel(count, x, out, near, far, held, send_lo, recv_lo, send_hi, recv_hi):
    outer, inner, me, hi, lo = place(count)
    rows = out.shape[0]
    meet("col", line_peers(count))

    def to_lo(d, e):
        h = lax.rem(hi + d, outer)
        l = lax.rem(lo + e, inner)
        return send(x.at[block(h * inner + l, rows)], near.at[d * (inner - 1) + e - 1],
                    send_lo.at[d, e - 1], recv_lo.at[d, e - 1], "col", hi * inner + l)

    def to_hi(d):
        return send(held.at[d - 1], far.at[d - 1], send_hi.at[d - 1], recv_hi.at[d - 1], "col",
                    lax.rem(hi + d, outer) * inner + lo)

    order = list(range(1, outer)) + [0]
    for d in order:
        for e in range(1, inner):
            to_lo(d, e).start()

    def local(d):
        h = lax.rem(hi + d, outer)
        return [(x, (h * inner + lo) * rows)] + [
            (near.at[d * (inner - 1) + e - 1], 0) for e in range(1, inner)
        ]

    for d in order:
        for e in range(1, inner):
            to_lo(d, e).wait_recv()
        if d:
            add_strips(held.at[d - 1], 0, local(d), rows)
            to_hi(d).start()
    for d in range(1, outer):
        to_hi(d).wait_recv()
    add_strips(out, 0, local(0) + [(far.at[d - 1], 0) for d in range(1, outer)], rows)
    for d in range(outer):
        for e in range(1, inner):
            to_lo(d, e).wait_send()
    for d in range(1, outer):
        to_hi(d).wait_send()


def row_kernel(count, parts, x, out, near, held, far, s1, r1, s2, r2, s3, r3):
    me = lax.axis_index("row")
    pairs = count // 2
    pair, side = lax.div(me, 2), lax.rem(me, 2)
    mate = pair * 2 + 1 - side
    others = [lax.rem(pair + d, pairs) * 2 + side for d in range(1, pairs)]
    meet("row", [mate] + others)
    rows = x.shape[0] // (2 * parts)

    def at(s, k):
        return block(s * parts + k, rows)

    def first(k):
        return send(x.at[at(1 - side, k)], near.at[k], s1.at[k], r1.at[k], "row", mate)

    def across(d, k):
        return send(held.at[k], far.at[(d - 1) * parts + k], s2.at[d - 1, k], r2.at[d - 1, k],
                    "row", others[d - 1])

    def back(k):
        return send(out.at[at(side, k)], out.at[at(side, k)], s3.at[k], r3.at[k], "row", mate)

    for k in range(parts):
        first(k).start()
    for k in range(parts):
        first(k).wait_recv()
        add_strips(held.at[k], 0, [(x, (side * parts + k) * rows), (near.at[k], 0)], rows)
        for d in range(1, pairs):
            across(d, k).start()
    for k in range(parts):
        for d in range(1, pairs):
            across(d, k).wait_recv()
        add_strips(out, (side * parts + k) * rows,
                   [(held.at[k], 0)] + [(far.at[(d - 1) * parts + k], 0) for d in range(1, pairs)],
                   rows)
        back(k).start()
    for k in range(parts):
        back(k).wait()
        first(k).wait_send()
        for d in range(1, pairs):
            across(d, k).wait_send()


def call(kernel, operands, outs, scratch, collective_id):
    spec = pl.BlockSpec(memory_space=pltpu.VMEM)
    return pl.pallas_call(
        kernel,
        out_shape=outs,
        in_specs=[spec] * len(operands),
        out_specs=jax.tree.map(lambda _: spec, outs),
        scratch_shapes=scratch,
        compiler_params=pltpu.CompilerParams(
            collective_id=collective_id, has_side_effects=True
        ),
    )(*operands)


def col_gather(x, collective_id):
    n = lax.axis_size("col")
    out = jax.ShapeDtypeStruct((x.shape[0] * n, x.shape[1]), x.dtype)
    return call(functools.partial(gather_kernel, n), [x], out, gather_sems(n), collective_id)


def col_gather_turn(x, tokens, collective_id):
    n = lax.axis_size("col")
    dma = pltpu.SemaphoreType.DMA
    outs = (
        jax.ShapeDtypeStruct((x.shape[0] * n, x.shape[1]), x.dtype),
        jax.ShapeDtypeStruct((tokens.shape[0] * n, tokens.shape[1] // n), tokens.dtype),
    )
    scratch = [dma((n - 1,)), dma((n - 1,))] + gather_sems(n)
    return call(functools.partial(gather_turn_kernel, n), [x, tokens], outs, scratch, collective_id)


def col_scatter(x, dtype, collective_id):
    n = lax.axis_size("col")
    outer, inner = split_of(n)
    rows, width = x.shape[0] // n, x.shape[1]
    dma = pltpu.SemaphoreType.DMA
    near = max(inner - 1, 1)
    scratch = [
        pltpu.VMEM((outer * near, rows, width), BF16),
        pltpu.VMEM((outer - 1, rows, width), BF16),
        pltpu.VMEM((outer - 1, rows, width), BF16),
        dma((outer, near)),
        dma((outer, near)),
        dma((outer - 1,)),
        dma((outer - 1,)),
    ]
    out = jax.ShapeDtypeStruct((rows, width), dtype)
    return call(functools.partial(scatter_kernel, n), [x], out, scratch, collective_id)


def row_sum(x, collective_id, parts=4):
    n = lax.axis_size("row")
    pairs = n // 2
    rows, width = x.shape[0] // (2 * parts), x.shape[1]
    dma = pltpu.SemaphoreType.DMA
    scratch = [
        pltpu.VMEM((parts, rows, width), BF16),
        pltpu.VMEM((parts, rows, width), BF16),
        pltpu.VMEM(((pairs - 1) * parts, rows, width), BF16),
        dma((parts,)),
        dma((parts,)),
        dma((pairs - 1, parts)),
        dma((pairs - 1, parts)),
        dma((parts,)),
        dma((parts,)),
    ]
    out = jax.ShapeDtypeStruct(x.shape, x.dtype)
    return call(functools.partial(row_kernel, n, parts), [x], out, scratch, collective_id)


def up_gradient(gate_pre, up_pre, target, factor):
    gate_act = jax.nn.silu(gate_pre)
    return ((gate_act * up_pre - target.astype(F32)) * gate_act * factor).astype(BF16)


def shards(tokens, left_proj, teacher_up, right_proj, student_gate, target):
    factor = 1.0 / math.sqrt(tokens.shape[0] * lax.axis_size("col"))
    picked, token_cols = col_gather_turn(mm(tokens, left_proj).astype(BF16), tokens, 0)
    gate_pre = mm(tokens, student_gate)
    features = row_sum(mm(picked, teacher_up).astype(BF16), 1)
    up_pre = col_scatter(mm(features, right_proj).astype(BF16), F32, 2)
    grad_up = up_gradient(gate_pre, up_pre, target, factor)
    grad_all = col_gather(grad_up, 3)
    back = row_sum(mm_nt(grad_all, right_proj).astype(BF16), 1)
    grad_right = mm_tn(features, grad_all)
    units = col_gather(col_scatter(mm_nt(back, teacher_up).astype(BF16), BF16, 4), 5)
    grad_left = mm_tn(token_cols, units)
    return (grad_left, grad_right)


def solution(mesh):
    return jax.shard_map(
        shards,
        mesh=mesh,
        in_specs=(
            P("col", None),
            P(None, "row"),
            P("row", "col"),
            P("col", "row"),
            P(None, "row"),
            P("col", "row"),
        ),
        out_specs=(P("col", "row"), P("col", "row")),
        check_vma=False,
    )
```

time: 557 us -> 447 us (0.80)
  waiting for transfers between devices: 438 us -> 0 us
  Pallas kernels: 0 us -> 361 us
  blocking collectives: 24.6 us -> 0 us
  between operations: 13.9 us -> 0.75 us
    pallas_call x0 -> x7, Pallas kernels: none -> 361 us  [call(): pl.pallas_call(kernel, out_shape=outs, in_specs=[spec] * len(operands), o...]
    all_gather x5 -> x0, waiting for transfers between devices: 204 us -> none  [the longest x1 69.7 us: shards(): grad_all = lax.all_gather(grad_up, 'col', axis=0, tiled=True)]
    reduce_scatter x3 -> x0, waiting for transfers between devices: 149 us -> none  [the longest x2 80.7 us: row_sum(): part = lax.psum_scatter(partial, 'row', scatter_dimension=0, tiled=True)]
    unnamed x10 -> x0, waiting for transfers between devices: 84.8 us -> none
    all_to_all x1 -> x0, blocking collectives: 24.6 us -> none  [shards(): lax.all_to_all(tokens, 'col', split_axis=1, concat_axis=0, tiled=True)]
    convert_element_type x0 -> x2, local copies, waits for them, and re-layouts: none -> 12.3 us  [the longest x1 6.13 us: shards(): features = row_sum(mm(picked, teacher_up).astype(BF16), 1)]
    unnamed x8 -> x13, local copies, waits for them, and re-layouts: 9.01 us -> 0.28 us
  transfers between devices with their start and end apart: 9 -> 0, of which waited for: 9 -> 0; matrix products, arithmetic and copies ran while one was open for 3% -> 0% of each run, Pallas kernels for 0% -> 0%
where the time goes in v2:
time: 447 us; the launch traced here: 444 us
  Pallas kernels  361 us (81%)
  matrix products  69.7 us (16%)
  local copies, waits for them, and re-layouts  12.6 us (3%)
    pallas_call x7, Pallas kernels, call(): pl.pallas_call(kernel, out_shape=outs, in_specs=[spec] * len(operands), o...  361 us
    dot_general x4, matrix products, mm(): return jnp.dot(a, b, preferred_element_type=F32)  32.7 us
    dot_general x2, matrix products, mm_nt(): lax.dot_general(a, b, (((1,), (1,)), ((), ())), preferred_element_type=F32)  19.6 us
    dot_general x2, matrix products, mm_tn(): lax.dot_general(a, b, (((0,), (0,)), ((), ())), preferred_element_type=F32)  17.4 us

profile of v2, /device:TPU:0, one launch (start us, length us, event | category | flops | bytes accessed | tf_op | source)
XLA Modules:
  0.0 444.4 jit_solution(7713859423182331232)
XLA Ops:
  0.6 3.8 convolution_convert_fusion.4.x
  4.4 52.0 %shard_map.77 = (bf16[1024,1024]{1,0:T(8,128)(2,1)}, bf16[1024,256]{1,0:T(8,128)(2,1)}) custom-call(bf16[128,1024]{1,0:T(8,128)(2,1)} %convolution_convert_fusion.4.x, bf16[128,2048]{1,0:T(8,128)(2,1)} %tokens.1), custom_call_target="tpu_custom_call" | custom-call | tf_op jit(solution)/shard_map/pallas_call | solution.py:232
  56.4 8.7 %convolution_convert_fusion.2 = bf16[1024,1856]{0,1:T(8,128)(2,1)} fusion(bf16[1024,1024]{1,0:T(8,128)(2,1)} %get-tuple-element.5, bf16[1024,1856]{0,1:T(8,128)(2,1)} %param.8), kind=kOutput, calls=%fused_computation.2 | convolution fusion | flops 3894214656 | bytes 9699328 | tf_op jit(solution)/shard_map/dot_general | solution.py:18
  65.1 6.1 %copy.17.x = bf16[1024,1856]{1,0:T(8,128)(2,1)} copy(bf16[1024,1856]{0,1:T(8,128)(2,1)} %convolution_convert_fusion.2) | data formatting | bytes 7602176 | tf_op jit(solution)/shard_map/convert_element_type | solution.py:309
  71.3 52.9 %shard_map.78 = bf16[1024,1856]{1,0:T(8,128)(2,1)} custom-call(bf16[1024,1856]{1,0:T(8,128)(2,1)} %copy.17.x), custom_call_target="tpu_custom_call" | custom-call | tf_op jit(solution)/shard_map/pallas_call | solution.py:232
  124.1 13.3 %convolution_convert_fusion.1 = bf16[1024,1856]{0,1:T(8,128)(2,1)} fusion(bf16[1024,1856]{1,0:T(8,128)(2,1)} %shard_map.78, bf16[1856,1856]{1,0:T(8,128)(2,1)} %param.9), kind=kOutput, calls=%fused_computation.1 | convolution fusion | flops 7056719872 | bytes 14491648 | tf_op jit(solution)/shard_map/dot_general | solution.py:18
  137.4 6.1 %copy.18.x = bf16[1024,1856]{1,0:T(8,128)(2,1)} copy(bf16[1024,1856]{0,1:T(8,128)(2,1)} %convolution_convert_fusion.1) | data formatting | bytes 7602176 | tf_op jit(solution)/shard_map/convert_element_type | solution.py:310
  143.6 64.4 %shard_map.79 = f32[128,1856]{1,0:T(8,128)} custom-call(bf16[1024,1856]{1,0:T(8,128)(2,1)} %copy.18.x), custom_call_target="tpu_custom_call" | custom-call | tf_op jit(solution)/shard_map/pallas_call | solution.py:232
  207.9 0.0 copy-done.3
  207.9 0.3 copy.19
  208.2 0.0 copy-done.1
  208.2 7.0 %multiply_convert_fusion.x = bf16[128,1856]{1,0:T(8,128)(2,1)} fusion(bf16[128,1856]{1,0:T(8,128)(2,1)S(1)} %copy.19, f32[128,1856]{1,0:T(8,128)} %shard_map.79, bf16[128,2048]{1,0:T(8,128)(2,1)S(1)} %copy-done.1, bf16[2048,1856]{0,1:T(8,128)(2,1)} %param.10), kind=kOutput, calls=%fused_computation.5 | convolution fusion | flops 975454208 | bytes 10027008 | tf_op jit(solution)/shard_map/dot_general | solution.py:18
  215.2 60.3 %shard_map.80 = bf16[1024,1856]{1,0:T(8,128)(2,1)} custom-call(bf16[128,1856]{1,0:T(8,128)(2,1)} %multiply_convert_fusion.x), custom_call_target="tpu_custom_call" | custom-call | tf_op jit(solution)/shard_map/pallas_call | solution.py:232
  275.5 0.0 copy-start
  275.5 0.0 slice-start.1
  275.5 14.1 %fusion.1 = f32[1856,1856]{1,0:T(8,128)} fusion(bf16[1024,1856]{1,0:T(8,128)(2,1)} %shard_map.78, bf16[1024,1856]{1,0:T(8,128)(2,1)} %shard_map.80), kind=kOutput, calls=%fused_computation.7 | convolution fusion | flops 7054819328 | bytes 21381120 | tf_op jit(solution)/shard_map/dot_general | solution.py:26
  289.6 0.0 slice-done
  289.6 10.5 %convolution_convert_fusion.x = bf16[1024,1856]{1,0:T(8,128)(2,1)} fusion(bf16[1024,1856]{1,0:T(8,128)(2,1)S(1)} %copy-done, bf16[1856,1856]{1,0:T(8,128)(2,1)S(1)} %bitcast.17), kind=kOutput, calls=%fused_computation | convolution fusion | flops 7056719872 | bytes 14491648 | tf_op jit(solution)/shard_map/dot_general | solution.py:22
  300.1 51.4 %shard_map.81 = bf16[1024,1856]{1,0:T(8,128)(2,1)} custom-call(bf16[1024,1856]{1,0:T(8,128)(2,1)} %convolution_convert_fusion.x), custom_call_target="tpu_custom_call" | custom-call | tf_op jit(solution)/shard_map/pallas_call | solution.py:232
  351.5 9.1 %convolution_convert_fusion.3.x = bf16[1024,1024]{1,0:T(8,128)(2,1)} fusion(bf16[1024,1856]{1,0:T(8,128)(2,1)} %shard_map.81, bf16[1024,1856]{0,1:T(8,128)(2,1)} %param.8), kind=kOutput, calls=%fused_computation.3 | convolution fusion | flops 3893362688 | bytes 9699328 | tf_op jit(solution)/shard_map/dot_general | solution.py:22
  360.6 44.9 %shard_map.82.x = bf16[128,1024]{1,0:T(8,128)(2,1)} custom-call(bf16[1024,1024]{1,0:T(8,128)(2,1)} %convolution_convert_fusion.3.x), custom_call_target="tpu_custom_call" | custom-call | tf_op jit(solution)/shard_map/pallas_call | solution.py:232
  405.5 35.6 %shard_map.83 = bf16[1024,1024]{1,0:T(8,128)(2,1)} custom-call(bf16[128,1024]{1,0:T(8,128)(2,1)} %shard_map.82.x), custom_call_target="tpu_custom_call" | custom-call | tf_op jit(solution)/shard_map/pallas_call | solution.py:232
  441.1 0.0 copy-done.2
  441.2 3.3 fusion
  (7 shorter events, 0.0 us)
Async XLA Ops:
  143.6 64.4 %copy-start.3 = (bf16[128,1856]{0,1:T(8,128)(2,1)S(1)}, bf16[128,1856]{0,1:T(8,128)(2,1)}, u32[]{:S(2)}) copy-start(bf16[128,1856]{0,1:T(8,128)(2,1)} %param.11) | copy-start | bytes 1425412
  143.6 64.6 %copy-start.1 = (bf16[128,2048]{1,0:T(8,128)(2,1)S(1)}, bf16[128,2048]{1,0:T(8,128)(2,1)}, u32[]{:S(2)}) copy-start(bf16[128,2048]{1,0:T(8,128)(2,1)} %tokens.1) | copy-start | bytes 1572868
  215.2 74.4 %slice-start = ((s8[7127040]{0:T(1024)(128)(4,1)}), s8[2932736]{0:T(1024)(128)(4,1)S(1)}, s32[]{:S(2)}) async-start(s8[7127040]{0:T(1024)(128)(4,1)} %bitcast.16), calls=%async_computation | async-start | bytes 5865472
  275.5 14.1 %copy-start = (bf16[1024,1856]{1,0:T(8,128)(2,1)S(1)}, bf16[1024,1856]{1,0:T(8,128)(2,1)}, u32[]{:S(2)}) copy-start(bf16[1024,1856]{1,0:T(8,128)(2,1)} %shard_map.80) | copy-start | bytes 11403268
  275.5 14.1 %slice-start.1 = ((s8[7127040]{0:T(1024)(128)(4,1)}), s8[4194304]{0:T(1024)(128)(4,1)S(1)}, s32[]{:S(2)}) async-start(s8[7127040]{0:T(1024)(128)(4,1)} %bitcast.16), calls=%async_computation.1 | async-start | bytes 8388608
  360.6 80.6 %copy-start.2 = (bf16[1024,256]{1,0:T(8,128)(2,1)S(1)}, bf16[1024,256]{1,0:T(8,128)(2,1)}, u32[]{:S(2)}) copy-start(bf16[1024,256]{1,0:T(8,128)(2,1)} %get-tuple-element.4) | copy-start | bytes 1572868

commit v3 on v2

v3 whole, which is shorter than its diff:
```python
import functools
import math

import jax
import jax.numpy as jnp
from jax import lax
from jax.experimental import pallas as pl
from jax.experimental.pallas import tpu as pltpu
from jax.experimental.layout import Layout, with_layout_constraint
from jax.sharding import PartitionSpec as P

MESH = pl.DeviceIdType.MESH
BF16 = jnp.bfloat16
F32 = jnp.float32
STRIP = 16


def mm(a, b):
    return jnp.dot(a, b, preferred_element_type=F32)


def mm_nt(a, b):
    return lax.dot_general(a, b, (((1,), (1,)), ((), ())), preferred_element_type=F32)


def mm_tn(a, b):
    return lax.dot_general(a, b, (((0,), (0,)), ((), ())), preferred_element_type=F32)


def short(x):
    return with_layout_constraint(x.astype(BF16), Layout((0, 1)))


def block(index, size):
    return pl.ds(pl.multiple_of(index * size, size), size)


def send(src, dst, send_sem, recv_sem, axis, peer):
    return pltpu.make_async_remote_copy(
        src_ref=src,
        dst_ref=dst,
        send_sem=send_sem,
        recv_sem=recv_sem,
        device_id={axis: peer},
        device_id_type=MESH,
    )


def add_strips(out, out_at, terms, rows):
    @pl.loop(0, rows // STRIP)
    def _(t):
        total = None
        for ref, at in terms:
            part = ref[pl.ds(pl.multiple_of(at + t * STRIP, STRIP), STRIP), :].astype(F32)
            total = part if total is None else total + part
        out[pl.ds(pl.multiple_of(out_at + t * STRIP, STRIP), STRIP), :] = total.astype(out.dtype)


def split_of(count):
    inner = 1
    while inner * inner * 4 <= count and count % (inner * 2) == 0:
        inner *= 2
    return count // inner, inner


def place(count):
    outer, inner = split_of(count)
    me = lax.axis_index("col")
    hi, lo = lax.div(me, inner), lax.rem(me, inner)
    return outer, inner, me, hi, lo


def line_peers(count):
    outer, inner, me, hi, lo = place(count)
    return [lax.rem(hi + d, outer) * inner + lo for d in range(1, outer)] + [
        hi * inner + lax.rem(lo + e, inner) for e in range(1, inner)
    ]


def all_peers(count):
    me = lax.axis_index("col")
    return [lax.rem(me + d, count) for d in range(1, count)]


def row_place(count):
    pairs = count // 2
    me = lax.axis_index("row")
    pair, side = lax.div(me, 2), lax.rem(me, 2)
    mate = pair * 2 + 1 - side
    others = [lax.rem(pair + d, pairs) * 2 + side for d in range(1, pairs)]
    return pairs, side, mate, others


def row_peers(count):
    pairs, side, mate, others = row_place(count)
    return [mate] + others


def meet(groups):
    barrier = pltpu.get_barrier_semaphore()
    total = 0
    for axis, peers in groups:
        for peer in peers:
            pl.semaphore_signal(barrier, inc=1, device_id={axis: peer}, device_id_type=MESH)
        total += len(peers)
    pl.semaphore_wait(barrier, total)


def gather_steps(count, x, out, send_hi, recv_hi, send_lo, recv_lo):
    outer, inner, me, hi, lo = place(count)
    rows = x.shape[0]

    def at(h, l):
        return block(h * inner + l, rows)

    def to_hi(d):
        return send(x, out.at[at(hi, lo)], send_hi.at[d - 1], recv_hi.at[d - 1], "col",
                    lax.rem(hi + d, outer) * inner + lo)

    def to_lo(d, e):
        h = lax.rem(hi + outer - d, outer)
        src = x if d == 0 else out.at[at(h, lo)]
        return send(src, out.at[at(h, lo)], send_lo.at[d, e - 1], recv_lo.at[d, e - 1], "col",
                    hi * inner + lax.rem(lo + e, inner))

    for e in range(1, inner):
        to_lo(0, e).start()
    for d in range(1, outer):
        to_hi(d).start()
    out[at(hi, lo), :] = x[...]
    yield
    for d in range(1, outer):
        to_hi(d).wait_recv()
        for e in range(1, inner):
            to_lo(d, e).start()
        yield
    for d in range(outer):
        for e in range(1, inner):
            to_lo(d, e).wait()
    for d in range(1, outer):
        to_hi(d).wait_send()


def scatter_steps(count, x, out, near, far, held, send_lo, recv_lo, send_hi, recv_hi):
    outer, inner, me, hi, lo = place(count)
    rows = out.shape[0]

    def to_lo(d, e):
        h = lax.rem(hi + d, outer)
        l = lax.rem(lo + e, inner)
        return send(x.at[block(h * inner + l, rows)], near.at[d * (inner - 1) + e - 1],
                    send_lo.at[d, e - 1], recv_lo.at[d, e - 1], "col", hi * inner + l)

    def to_hi(d):
        return send(held.at[d - 1], far.at[d - 1], send_hi.at[d - 1], recv_hi.at[d - 1], "col",
                    lax.rem(hi + d, outer) * inner + lo)

    order = list(range(1, outer)) + [0]
    for d in order:
        for e in range(1, inner):
            to_lo(d, e).start()
    yield

    def local(d):
        h = lax.rem(hi + d, outer)
        return [(x, (h * inner + lo) * rows)] + [
            (near.at[d * (inner - 1) + e - 1], 0) for e in range(1, inner)
        ]

    for d in order:
        for e in range(1, inner):
            to_lo(d, e).wait_recv()
        if d:
            add_strips(held.at[d - 1], 0, local(d), rows)
            to_hi(d).start()
        yield
    for d in range(1, outer):
        to_hi(d).wait_recv()
    add_strips(out, 0, local(0) + [(far.at[d - 1], 0) for d in range(1, outer)], rows)
    yield
    for d in range(outer):
        for e in range(1, inner):
            to_lo(d, e).wait_send()
    for d in range(1, outer):
        to_hi(d).wait_send()


def turn_steps(count, tokens, turned, turn_send, turn_recv):
    me = lax.axis_index("col")
    width, rows = turned.shape[1], tokens.shape[0] // 2

    def turn(d, half):
        peer = lax.rem(me + d, count)
        return send(tokens.at[pl.ds(half * rows, rows), block(peer, width)],
                    turned.at[block(half * count + me, rows)],
                    turn_send.at[d - 1, half], turn_recv.at[d - 1, half], "col", peer)

    yield
    for half in range(2):
        for d in range(1, count):
            turn(d, half).start()
        turned[block(half * count + me, rows), :] = tokens[
            pl.ds(half * rows, rows), block(me, width)
        ]
    yield
    yield
    yield
    for half in range(2):
        for d in range(1, count):
            turn(d, half).wait()


def row_steps(count, parts, x, out, near, held, far, s1, r1, s2, r2, s3, r3):
    pairs, side, mate, others = row_place(count)
    rows = x.shape[0] // (2 * parts)

    def at(s, k):
        return block(s * parts + k, rows)

    def first(k):
        return send(x.at[at(1 - side, k)], near.at[k], s1.at[k], r1.at[k], "row", mate)

    def across(d, k):
        return send(held.at[k], far.at[(d - 1) * parts + k], s2.at[d - 1, k], r2.at[d - 1, k],
                    "row", others[d - 1])

    def back(k):
        return send(out.at[at(side, k)], out.at[at(side, k)], s3.at[k], r3.at[k], "row", mate)

    for k in range(parts):
        first(k).start()
    yield
    for k in range(parts):
        first(k).wait_recv()
        add_strips(held.at[k], 0, [(x, (side * parts + k) * rows), (near.at[k], 0)], rows)
        for d in range(1, pairs):
            across(d, k).start()
        yield
    for k in range(parts):
        for d in range(1, pairs):
            across(d, k).wait_recv()
        add_strips(out, (side * parts + k) * rows,
                   [(held.at[k], 0)] + [(far.at[(d - 1) * parts + k], 0) for d in range(1, pairs)],
                   rows)
        back(k).start()
        yield
    for k in range(parts):
        back(k).wait()
        first(k).wait_send()
        for d in range(1, pairs):
            across(d, k).wait_send()


def like(rows, width, dtype):
    return jax.ShapeDtypeStruct((rows, width), dtype)


def gather_sems(count):
    outer, inner = split_of(count)
    dma = pltpu.SemaphoreType.DMA
    far, near = (outer - 1,), (outer, max(inner - 1, 1))
    return [dma(far), dma(far), dma(near), dma(near)]


def scatter_scratch(count, rows, width):
    outer, inner = split_of(count)
    dma = pltpu.SemaphoreType.DMA
    near = max(inner - 1, 1)
    return [
        pltpu.VMEM((outer * near, rows, width), BF16),
        pltpu.VMEM((outer - 1, rows, width), BF16),
        pltpu.VMEM((outer - 1, rows, width), BF16),
        dma((outer, near)),
        dma((outer, near)),
        dma((outer - 1,)),
        dma((outer - 1,)),
    ]


def gather(x):
    n = lax.axis_size("col")
    out = like(x.shape[0] * n, x.shape[1], x.dtype)
    return "line", x, out, gather_sems(n), functools.partial(gather_steps, n)


def scatter(x, dtype):
    n = lax.axis_size("col")
    rows, width = x.shape[0] // n, x.shape[1]
    out = like(rows, width, dtype)
    return "line", x, out, scatter_scratch(n, rows, width), functools.partial(scatter_steps, n)


def col_sum(x):
    n = lax.axis_size("col")
    rows, width = x.shape[0] // n, x.shape[1]
    scratch = scatter_scratch(n, rows, width)

    def steps(x, out, total, *scr):
        yield from scatter_steps(n, x, total, *scr[: len(scratch)])
        yield from gather_steps(n, total, out, *scr[len(scratch) :])

    every = [pltpu.VMEM((rows, width), BF16)] + scratch + gather_sems(n)
    return "line", x, like(*x.shape, x.dtype), every, steps


def turn(tokens):
    n = lax.axis_size("col")
    dma = pltpu.SemaphoreType.DMA
    out = like(tokens.shape[0] * n, tokens.shape[1] // n, tokens.dtype)
    sems = [dma((n - 1, 2)), dma((n - 1, 2))]
    return "all", tokens, out, sems, functools.partial(turn_steps, n)


def row_sum(x, parts=4):
    n = lax.axis_size("row")
    pairs = n // 2
    rows, width = x.shape[0] // (2 * parts), x.shape[1]
    dma = pltpu.SemaphoreType.DMA
    scratch = [
        pltpu.VMEM((parts, rows, width), BF16),
        pltpu.VMEM((parts, rows, width), BF16),
        pltpu.VMEM(((pairs - 1) * parts, rows, width), BF16),
        dma((parts,)),
        dma((parts,)),
        dma((pairs - 1, parts)),
        dma((pairs - 1, parts)),
        dma((parts,)),
        dma((parts,)),
    ]
    return "row", x, like(*x.shape, x.dtype), scratch, functools.partial(row_steps, n, parts)


def together(collective_id, *ops):
    kinds = {op[0] for op in ops}
    col, row = lax.axis_size("col"), lax.axis_size("row")

    def kernel(*refs):
        groups = []
        if "all" in kinds:
            groups.append(("col", all_peers(col)))
        elif "line" in kinds:
            groups.append(("col", line_peers(col)))
        if "row" in kinds:
            groups.append(("row", row_peers(row)))
        meet(groups)
        n = len(ops)
        at = 2 * n
        running = []
        for i, op in enumerate(ops):
            scratch = refs[at : at + len(op[3])]
            at += len(op[3])
            running.append(op[4](refs[i], refs[n + i], *scratch))
        while running:
            running = [steps for steps in running if next(steps, running) is not running]

    spec = pl.BlockSpec(memory_space=pltpu.VMEM)
    return pl.pallas_call(
        kernel,
        out_shape=[op[2] for op in ops],
        in_specs=[spec] * len(ops),
        out_specs=[spec] * len(ops),
        scratch_shapes=[item for op in ops for item in op[3]],
        compiler_params=pltpu.CompilerParams(
            collective_id=collective_id, has_side_effects=True
        ),
    )(*[op[1] for op in ops])


def up_gradient(gate_pre, up_pre, target, factor):
    gate_act = jax.nn.silu(gate_pre)
    return ((gate_act * up_pre - target.astype(F32)) * gate_act * factor).astype(BF16)


def shards(tokens, left_proj, teacher_up, right_proj, student_gate, target):
    factor = 1.0 / math.sqrt(tokens.shape[0] * lax.axis_size("col"))
    half = tokens.shape[0] // 2

    def up(x):
        return short(mm(x, right_proj))

    def down(x):
        return short(mm_nt(x, right_proj))

    picked = short(mm(tokens, left_proj))
    picked_a, token_cols = together(0, gather(picked[:half]), turn(tokens))
    gate_pre = mm(tokens, student_gate)
    features_a, picked_b = together(
        1, row_sum(short(mm(picked_a, teacher_up))), gather(picked[half:])
    )
    features_b, up_a = together(
        2, row_sum(short(mm(picked_b, teacher_up))), scatter(up(features_a), F32)
    )
    grad_a = up_gradient(gate_pre[:half], up_a, target[:half], factor)
    up_b, all_a = together(3, scatter(up(features_b), F32), gather(grad_a))
    grad_b = up_gradient(gate_pre[half:], up_b, target[half:], factor)
    back_a, all_b = together(4, row_sum(down(all_a)), gather(grad_b))
    back_b, units_a = together(
        5, row_sum(down(all_b)), col_sum(short(mm_nt(back_a, teacher_up)))
    )
    grad_right = mm_tn(
        jnp.concatenate([features_a, features_b]), jnp.concatenate([all_a, all_b])
    )
    (units_b,) = together(6, col_sum(short(mm_nt(back_b, teacher_up))))
    grad_left = mm_tn(token_cols, jnp.concatenate([units_a, units_b]))
    return (grad_left, grad_right)


def solution(mesh):
    return jax.shard_map(
        shards,
        mesh=mesh,
        in_specs=(
            P("col", None),
            P(None, "row"),
            P("row", "col"),
            P("col", "row"),
            P(None, "row"),
            P("col", "row"),
        ),
        out_specs=(P("col", "row"), P("col", "row")),
        check_vma=False,
    )
```

time: 447 us -> 363 us (0.81)
  Pallas kernels: 361 us -> 274 us
  matrix products: 69.7 us -> 82.3 us
  local copies, waits for them, and re-layouts: 12.6 us -> 1.39 us
    pallas_call x7, Pallas kernels: 361 us -> 274 us  [together(): pl.pallas_call(kernel, out_shape=[op[2] for op in ops], in_specs=[spec] *...]
    convert_element_type x2 -> x0, local copies, waits for them, and re-layouts: 12.3 us -> none  [the longest x1 6.13 us: shards(): features = row_sum(mm(picked, teacher_up).astype(BF16), 1)]
    dot_general x2 -> x4, matrix products: 19.6 us -> 27.2 us  [mm_nt(): lax.dot_general(a, b, (((1,), (1,)), ((), ())), preferred_element_type=F32)]
    dot_general x4 -> x6, matrix products: 32.7 us -> 39.2 us  [mm(): return jnp.dot(a, b, preferred_element_type=F32)]
where the time goes in v3:
time: 363 us
  Pallas kernels  274 us (75%)
  matrix products  82.3 us (23%)
  other arithmetic  3.83 us (1%)
    pallas_call x7, Pallas kernels, together(): pl.pallas_call(kernel, out_shape=[op[2] for op in ops], in_specs=[spec] *...  274 us
    dot_general x6, matrix products, mm(): return jnp.dot(a, b, preferred_element_type=F32)  39.2 us
    dot_general x4, matrix products, mm_nt(): lax.dot_general(a, b, (((1,), (1,)), ((), ())), preferred_element_type=F32)  27.2 us
    dot_general x2, matrix products, mm_tn(): lax.dot_general(a, b, (((0,), (0,)), ((), ())), preferred_element_type=F32)  15.9 us

profile of v3, /device:TPU:0, one launch (start us, length us, event | category | flops | bytes accessed | tf_op | source)
XLA Modules:
  0.0 362.7 jit_solution(6214065547787766420)
XLA Ops:
  0.7 3.1 convolution_convert_fusion.8
  3.8 0.7 fusion.14
  4.7 0.2 copy.14
  4.9 0.2 copy.13
  5.2 5.8 %fusion.15 = f32[128,1856]{1,0:T(8,128)S(1)} fusion(bf16[128,2048]{1,0:T(8,128)(2,1)S(1)} %copy-done, bf16[2048,1856]{0,1:T(8,128)(2,1)} %param.10), kind=kOutput, calls=%fused_computation.26 | convolution fusion | flops 973078528 | bytes 9076736 | tf_op jit(solution)/shard_map/dot_general | solution.py:19
  11.0 30.2 %shard_map.77 = (bf16[512,1024]{1,0:T(8,128)(2,1)}, bf16[1024,256]{1,0:T(8,128)(2,1)}) custom-call(bf16[64,1024]{1,0:T(8,128)(2,1)} %get-tuple-element.29.refs_0_, bf16[128,2048]{1,0:T(8,128)(2,1)} %refs_1_.1), custom_call_target="tpu_custom_call" | custom-call | tf_op jit(solution)/shard_map/pallas_call | solution.py:357
  41.2 6.0 %convolution_convert_fusion.5.refs_0_ = bf16[512,1856]{1,0:T(8,128)(2,1)} fusion(bf16[512,1024]{1,0:T(8,128)(2,1)} %get-tuple-element.15, bf16[1024,1856]{0,1:T(8,128)(2,1)} %param.8), kind=kOutput, calls=%fused_computation.12 | convolution fusion | flops 1947107328 | bytes 6750208 | tf_op jit(solution)/shard_map/dot_general | solution.py:19
  47.2 34.4 %shard_map.78 = (bf16[512,1856]{1,0:T(8,128)(2,1)}, bf16[512,1024]{1,0:T(8,128)(2,1)}) custom-call(bf16[512,1856]{1,0:T(8,128)(2,1)} %convolution_convert_fusion.5.refs_0_, bf16[64,1024]{1,0:T(8,128)(2,1)} %get-tuple-element.28.refs_1_), custom_call_target="tpu_custom_call" | custom-call | tf_op jit(solution)/shard_map/pallas_call | solution.py:357
  81.7 6.2 %convolution_convert_fusion.4.refs_0_ = bf16[512,1856]{1,0:T(8,128)(2,1)} fusion(bf16[512,1024]{1,0:T(8,128)(2,1)} %get-tuple-element.16, bf16[1024,1856]{0,1:T(8,128)(2,1)} %param.8), kind=kOutput, calls=%fused_computation.11 | convolution fusion | flops 1947107328 | bytes 6750208 | tf_op jit(solution)/shard_map/dot_general | solution.py:19
  87.9 8.6 %convolution_convert_fusion.3.refs_1_ = bf16[512,1856]{1,0:T(8,128)(2,1)} fusion(bf16[512,1856]{1,0:T(8,128)(2,1)S(1)} %copy-done.2, bf16[1856,1856]{1,0:T(8,128)(2,1)} %param.9), kind=kOutput, calls=%fused_computation.10 | convolution fusion | flops 3528359936 | bytes 10690560 | tf_op jit(solution)/shard_map/dot_general | solution.py:19
  96.5 37.2 %shard_map.79 = (bf16[512,1856]{1,0:T(8,128)(2,1)}, f32[64,1856]{1,0:T(8,128)}) custom-call(bf16[512,1856]{1,0:T(8,128)(2,1)} %convolution_convert_fusion.4.refs_0_, bf16[512,1856]{1,0:T(8,128)(2,1)} %convolution_convert_fusion.3.refs_1_), custom_call_target="tpu_custom_call" | custom-call | tf_op jit(solution)/shard_map/pallas_call | solution.py:357
  133.7 1.9 multiply_convert_fusion.1.refs_1_
  135.6 9.4 %convolution_convert_fusion.2.refs_0_ = bf16[512,1856]{1,0:T(8,128)(2,1)} fusion(bf16[512,1856]{1,0:T(8,128)(2,1)} %get-tuple-element.18, bf16[1856,1856]{1,0:T(8,128)(2,1)} %param.9), kind=kOutput, calls=%fused_computation.9 | convolution fusion | flops 3528359936 | bytes 10690560 | tf_op jit(solution)/shard_map/dot_general | solution.py:19
  145.0 50.0 %shard_map.80 = (f32[64,1856]{1,0:T(8,128)}, bf16[512,1856]{1,0:T(8,128)(2,1)}) custom-call(bf16[512,1856]{1,0:T(8,128)(2,1)} %convolution_convert_fusion.2.refs_0_, bf16[64,1856]{1,0:T(8,128)(2,1)} %multiply_convert_fusion.1.refs_1_), custom_call_target="tpu_custom_call" | custom-call | tf_op jit(solution)/shard_map/pallas_call | solution.py:357
  195.1 1.9 multiply_convert_fusion.refs_1_
  197.0 9.4 %convolution_convert_fusion.1.refs_0_ = bf16[512,1856]{1,0:T(8,128)(2,1)} fusion(bf16[512,1856]{1,0:T(8,128)(2,1)} %get-tuple-element.20, bf16[1856,1856]{1,0:T(8,128)(2,1)} %param.9), kind=kOutput, calls=%fused_computation.8 | convolution fusion | flops 3528359936 | bytes 10690560 | tf_op jit(solution)/shard_map/dot_general | solution.py:23
  206.4 36.7 %shard_map.81 = (bf16[512,1856]{1,0:T(8,128)(2,1)}, bf16[512,1856]{1,0:T(8,128)(2,1)}) custom-call(bf16[512,1856]{1,0:T(8,128)(2,1)} %convolution_convert_fusion.1.refs_0_, bf16[64,1856]{1,0:T(8,128)(2,1)} %multiply_convert_fusion.refs_1_), custom_call_target="tpu_custom_call" | custom-call | tf_op jit(solution)/shard_map/pallas_call | solution.py:357
  243.1 6.1 %convolution_convert_fusion.7.refs_1_ = bf16[512,1024]{1,0:T(8,128)(2,1)} fusion(bf16[512,1856]{1,0:T(8,128)(2,1)} %get-tuple-element.23, bf16[1024,1856]{0,1:T(8,128)(2,1)} %param.8), kind=kOutput, calls=%fused_computation.18 | convolution fusion | flops 1946681344 | bytes 6750208 | tf_op jit(solution)/shard_map/dot_general | solution.py:23
  249.2 5.7 %convolution_convert_fusion.refs_0_ = bf16[512,1856]{1,0:T(8,128)(2,1)} fusion(bf16[512,1856]{1,0:T(8,128)(2,1)S(1)} %copy-done.6, bf16[1856,1856]{1,0:T(8,128)(2,1)S(1)} %bitcast.22), kind=kOutput, calls=%fused_computation.7 | convolution fusion | flops 3528359936 | bytes 10690560 | tf_op jit(solution)/shard_map/dot_general | solution.py:23
  254.9 44.7 %shard_map.82 = (bf16[512,1856]{1,0:T(8,128)(2,1)}, bf16[512,1024]{1,0:T(8,128)(2,1)}) custom-call(bf16[512,1856]{1,0:T(8,128)(2,1)} %convolution_convert_fusion.refs_0_, bf16[512,1024]{1,0:T(8,128)(2,1)} %convolution_convert_fusion.7.refs_1_), custom_call_target="tpu_custom_call" | custom-call | tf_op jit(solution)/shard_map/pallas_call | solution.py:357
  299.6 6.1 %convolution_convert_fusion.6.refs_0_ = bf16[512,1024]{1,0:T(8,128)(2,1)} fusion(bf16[512,1856]{1,0:T(8,128)(2,1)} %get-tuple-element.25, bf16[1024,1856]{0,1:T(8,128)(2,1)} %param.8), kind=kOutput, calls=%fused_computation.17 | convolution fusion | flops 1946681344 | bytes 6750208 | tf_op jit(solution)/shard_map/dot_general | solution.py:23
  305.7 41.0 %shard_map.83 = bf16[512,1024]{1,0:T(8,128)(2,1)} custom-call(bf16[512,1024]{1,0:T(8,128)(2,1)} %convolution_convert_fusion.6.refs_0_), custom_call_target="tpu_custom_call" | custom-call | tf_op jit(solution)/shard_map/pallas_call | solution.py:357
  346.8 3.1 fusion.7
  349.9 12.8 %fusion = f32[1856,1856]{1,0:T(8,128)} fusion(bf16[512,1856]{1,0:T(8,128)(2,1)S(1)} %copy-done.4, bf16[512,1856]{1,0:T(8,128)(2,1)S(1)} %copy-done.3, bf16[512,1856]{1,0:T(8,128)(2,1)} %get-tuple-element.22, bf16[512,1856]{1,0:T(8,128)(2,1)S(1)} %copy-done.5), kind=kOutput, calls=%fused_computation | convolution fusion | flops 7070023680 | bytes 21381120 | tf_op jit(solution)/shard_map/dot_general | solution.py:27
  (24 shorter events, 0.2 us)
Async XLA Ops:
  0.6 4.5 %copy-start = (bf16[128,2048]{1,0:T(8,128)(2,1)S(1)}, bf16[128,2048]{1,0:T(8,128)(2,1)}, u32[]{:S(2)}) copy-start(bf16[128,2048]{1,0:T(8,128)(2,1)} %refs_1_.1) | copy-start | bytes 1572868
  0.6 3.9 %copy-start.1 = (bf16[128,1856]{0,1:T(8,128)(2,1)S(1)}, bf16[128,1856]{0,1:T(8,128)(2,1)}, u32[]{:S(2)}) copy-start(bf16[128,1856]{0,1:T(8,128)(2,1)} %param.11) | copy-start | bytes 1425412
  81.7 6.2 %copy-start.2 = (bf16[512,1856]{1,0:T(8,128)(2,1)S(1)}, bf16[512,1856]{1,0:T(8,128)(2,1)}, u32[]{:S(2)}) copy-start(bf16[512,1856]{1,0:T(8,128)(2,1)} %get-tuple-element.17) | copy-start | bytes 5701636
  206.3 42.8 %slice-start = ((s8[7127040]{0:T(1024)(128)(4,1)}), s8[2932736]{0:T(1024)(128)(4,1)S(1)}, s32[]{:S(2)}) async-start(s8[7127040]{0:T(1024)(128)(4,1)} %bitcast.21), calls=%async_computation | async-start | bytes 5865472
  243.0 6.1 %slice-start.1 = ((s8[7127040]{0:T(1024)(128)(4,1)}), s8[4194304]{0:T(1024)(128)(4,1)S(1)}, s32[]{:S(2)}) async-start(s8[7127040]{0:T(1024)(128)(4,1)} %bitcast.21), calls=%async_computation.1 | async-start | bytes 8388608
  243.1 6.1 %copy-start.6 = (bf16[512,1856]{1,0:T(8,128)(2,1)S(1)}, bf16[512,1856]{1,0:T(8,128)(2,1)}, u32[]{:S(2)}) copy-start(bf16[512,1856]{1,0:T(8,128)(2,1)} %get-tuple-element.22) | copy-start | bytes 5701636
  299.6 47.2 %copy-start.7 = (bf16[512,1024]{1,0:T(8,128)(2,1)S(1)}, bf16[512,1024]{1,0:T(8,128)(2,1)}, u32[]{:S(2)}) copy-start(bf16[512,1024]{1,0:T(8,128)(2,1)} %get-tuple-element.24) | copy-start | bytes 3145732
  299.6 47.2 %copy-start.8 = (bf16[1024,256]{1,0:T(8,128)(2,1)S(1)}, bf16[1024,256]{1,0:T(8,128)(2,1)}, u32[]{:S(2)}) copy-start(bf16[1024,256]{1,0:T(8,128)(2,1)} %get-tuple-element.14) | copy-start | bytes 1572868
  305.7 44.2 %copy-start.3 = (bf16[512,1856]{1,0:T(8,128)(2,1)S(1)}, bf16[512,1856]{1,0:T(8,128)(2,1)}, u32[]{:S(2)}) copy-start(bf16[512,1856]{1,0:T(8,128)(2,1)} %get-tuple-element.17) | copy-start | bytes 5701636
  346.8 3.1 copy-start.4
  346.8 3.1 copy-start.5

commit v4 on v3

--- a/solution.py
+++ b/solution.py
@@ -202,8 +202,6 @@
         turned[block(half * count + me, rows), :] = tokens[
             pl.ds(half * rows, rows), block(me, width)
         ]
-    yield
-    yield
     yield
     for half in range(2):
         for d in range(1, count):
@@ -280,14 +278,15 @@
 def gather(x):
     n = lax.axis_size("col")
     out = like(x.shape[0] * n, x.shape[1], x.dtype)
-    return "line", x, out, gather_sems(n), functools.partial(gather_steps, n)
+    return "line", x, out, gather_sems(n), functools.partial(gather_steps, n), split_of(n)[0] + 1
 
 
 def scatter(x, dtype):
     n = lax.axis_size("col")
     rows, width = x.shape[0] // n, x.shape[1]
     out = like(rows, width, dtype)
-    return "line", x, out, scatter_scratch(n, rows, width), functools.partial(scatter_steps, n)
+    steps = functools.partial(scatter_steps, n)
+    return "line", x, out, scatter_scratch(n, rows, width), steps, split_of(n)[0] + 3
 
 
 def col_sum(x):
@@ -300,7 +299,7 @@
         yield from gather_steps(n, total, out, *scr[len(scratch) :])
 
     every = [pltpu.VMEM((rows, width), BF16)] + scratch + gather_sems(n)
-    return "line", x, like(*x.shape, x.dtype), every, steps
+    return "line", x, like(*x.shape, x.dtype), every, steps, 2 * split_of(n)[0] + 3
 
 
 def turn(tokens):
@@ -308,10 +307,10 @@
     dma = pltpu.SemaphoreType.DMA
     out = like(tokens.shape[0] * n, tokens.shape[1] // n, tokens.dtype)
     sems = [dma((n - 1, 2)), dma((n - 1, 2))]
-    return "all", tokens, out, sems, functools.partial(turn_steps, n)
-
-
-def row_sum(x, parts=4):
+    return "all", tokens, out, sems, functools.partial(turn_steps, n), 3
+
+
+def row_sum(x, parts=8):
     n = lax.axis_size("row")
     pairs = n // 2
     rows, width = x.shape[0] // (2 * parts), x.shape[1]
@@ -327,7 +326,8 @@
         dma((parts,)),
         dma((parts,)),
     ]
-    return "row", x, like(*x.shape, x.dtype), scratch, functools.partial(row_steps, n, parts)
+    steps = functools.partial(row_steps, n, parts)
+    return "row", x, like(*x.shape, x.dtype), scratch, steps, 2 * parts + 2
 
 
 def together(collective_id, *ops):
@@ -350,8 +350,16 @@
             scratch = refs[at : at + len(op[3])]
             at += len(op[3])
             running.append(op[4](refs[i], refs[n + i], *scratch))
-        while running:
-            running = [steps for steps in running if next(steps, running) is not running]
+        for steps in running:
+            next(steps)
+        taken = [1] * n
+        while any(running):
+            i = min(
+                (i for i in range(n) if running[i]), key=lambda i: (taken[i] + 1) / ops[i][5]
+            )
+            taken[i] += 1
+            if next(running[i], "end") == "end":
+                running[i] = None
 
     spec = pl.BlockSpec(memory_space=pltpu.VMEM)
     return pl.pallas_call(
@@ -382,10 +390,10 @@
         return short(mm_nt(x, right_proj))
 
     picked = short(mm(tokens, left_proj))
-    picked_a, token_cols = together(0, gather(picked[:half]), turn(tokens))
+    (picked_a,) = together(0, gather(picked[:half]))
     gate_pre = mm(tokens, student_gate)
-    features_a, picked_b = together(
-        1, row_sum(short(mm(picked_a, teacher_up))), gather(picked[half:])
+    features_a, picked_b, token_cols = together(
+        1, row_sum(short(mm(picked_a, teacher_up))), gather(picked[half:]), turn(tokens)
     )
     features_b, up_a = together(
         2, row_sum(short(mm(picked_b, teacher_up))), scatter(up(features_a), F32)

time: 363 us -> 346 us (0.953)
  Pallas kernels: 274 us -> 257 us
    pallas_call x7, Pallas kernels: 274 us -> 257 us  [together(): pl.pallas_call(kernel, out_shape=[op[2] for op in ops], in_specs=[spec] *...]
where the time goes in v4:
time: 346 us; the launch traced here: 345 us
  Pallas kernels  257 us (74%)
  matrix products  82.3 us (24%)
  other arithmetic  3.83 us (1%)
    pallas_call x7, Pallas kernels, together(): pl.pallas_call(kernel, out_shape=[op[2] for op in ops], in_specs=[spec] *...  257 us
    dot_general x6, matrix products, mm(): return jnp.dot(a, b, preferred_element_type=F32)  39.2 us
    dot_general x4, matrix products, mm_nt(): lax.dot_general(a, b, (((1,), (1,)), ((), ())), preferred_element_type=F32)  27.2 us
    dot_general x2, matrix products, mm_tn(): lax.dot_general(a, b, (((0,), (0,)), ((), ())), preferred_element_type=F32)  15.9 us

profile of v4, /device:TPU:0, one launch (start us, length us, event | category | flops | bytes accessed | tf_op | source)
XLA Modules:
  0.0 345.2 jit_solution(3122185859894457674)
XLA Ops:
  0.7 3.1 convolution_convert_fusion.8
  3.8 0.7 fusion.14
  4.7 0.2 copy.14
  4.9 0.2 copy.13
  5.2 5.8 %fusion.15 = f32[128,1856]{1,0:T(8,128)S(1)} fusion(bf16[128,2048]{1,0:T(8,128)(2,1)S(1)} %copy-done, bf16[2048,1856]{0,1:T(8,128)(2,1)} %param.10), kind=kOutput, calls=%fused_computation.26 | convolution fusion | flops 973078528 | bytes 9076736 | tf_op jit(solution)/shard_map/dot_general | solution.py:19
  11.0 24.5 %shard_map.77 = bf16[512,1024]{1,0:T(8,128)(2,1)} custom-call(bf16[64,1024]{1,0:T(8,128)(2,1)} %get-tuple-element.27.refs_0_), custom_call_target="tpu_custom_call" | custom-call | tf_op jit(solution)/shard_map/pallas_call | solution.py:365
  35.4 6.0 %convolution_convert_fusion.5.refs_0_ = bf16[512,1856]{1,0:T(8,128)(2,1)} fusion(bf16[512,1024]{1,0:T(8,128)(2,1)} %shard_map.77, bf16[1024,1856]{0,1:T(8,128)(2,1)} %param.8), kind=kOutput, calls=%fused_computation.12 | convolution fusion | flops 1947107328 | bytes 6750208 | tf_op jit(solution)/shard_map/dot_general | solution.py:19
  41.5 33.5 %shard_map.78 = (bf16[512,1856]{1,0:T(8,128)(2,1)}, bf16[512,1024]{1,0:T(8,128)(2,1)}, bf16[1024,256]{1,0:T(8,128)(2,1)}) custom-call(bf16[512,1856]{1,0:T(8,128)(2,1)} %convolution_convert_fusion.5.refs_0_, bf16[64,1024]{1,0:T(8,128)(2,1)} %get-tuple-element.26.refs_1_, bf16[128,2048]{1,0:T(8,128)(2,1)} %refs_2_.1), custom_call_target="tpu_custom_call" | custom-call | tf_op jit(solution)/shard_map/pallas_call | solution.py:365
  75.0 6.2 %convolution_convert_fusion.4.refs_0_ = bf16[512,1856]{1,0:T(8,128)(2,1)} fusion(bf16[512,1024]{1,0:T(8,128)(2,1)} %get-tuple-element.14, bf16[1024,1856]{0,1:T(8,128)(2,1)} %param.8), kind=kOutput, calls=%fused_computation.11 | convolution fusion | flops 1947107328 | bytes 6750208 | tf_op jit(solution)/shard_map/dot_general | solution.py:19
  81.2 8.6 %convolution_convert_fusion.3.refs_1_ = bf16[512,1856]{1,0:T(8,128)(2,1)} fusion(bf16[512,1856]{1,0:T(8,128)(2,1)S(1)} %copy-done.2, bf16[1856,1856]{1,0:T(8,128)(2,1)} %param.9), kind=kOutput, calls=%fused_computation.10 | convolution fusion | flops 3528359936 | bytes 10690560 | tf_op jit(solution)/shard_map/dot_general | solution.py:19
  89.8 36.3 %shard_map.79 = (bf16[512,1856]{1,0:T(8,128)(2,1)}, f32[64,1856]{1,0:T(8,128)}) custom-call(bf16[512,1856]{1,0:T(8,128)(2,1)} %convolution_convert_fusion.4.refs_0_, bf16[512,1856]{1,0:T(8,128)(2,1)} %convolution_convert_fusion.3.refs_1_), custom_call_target="tpu_custom_call" | custom-call | tf_op jit(solution)/shard_map/pallas_call | solution.py:365
  126.1 1.9 multiply_convert_fusion.1.refs_1_
  128.0 9.4 %convolution_convert_fusion.2.refs_0_ = bf16[512,1856]{1,0:T(8,128)(2,1)} fusion(bf16[512,1856]{1,0:T(8,128)(2,1)} %get-tuple-element.16, bf16[1856,1856]{1,0:T(8,128)(2,1)} %param.9), kind=kOutput, calls=%fused_computation.9 | convolution fusion | flops 3528359936 | bytes 10690560 | tf_op jit(solution)/shard_map/dot_general | solution.py:19
  137.4 49.4 %shard_map.80 = (f32[64,1856]{1,0:T(8,128)}, bf16[512,1856]{1,0:T(8,128)(2,1)}) custom-call(bf16[512,1856]{1,0:T(8,128)(2,1)} %convolution_convert_fusion.2.refs_0_, bf16[64,1856]{1,0:T(8,128)(2,1)} %multiply_convert_fusion.1.refs_1_), custom_call_target="tpu_custom_call" | custom-call | tf_op jit(solution)/shard_map/pallas_call | solution.py:365
  186.8 1.9 multiply_convert_fusion.refs_1_
  188.7 9.4 %convolution_convert_fusion.1.refs_0_ = bf16[512,1856]{1,0:T(8,128)(2,1)} fusion(bf16[512,1856]{1,0:T(8,128)(2,1)} %get-tuple-element.18, bf16[1856,1856]{1,0:T(8,128)(2,1)} %param.9), kind=kOutput, calls=%fused_computation.8 | convolution fusion | flops 3528359936 | bytes 10690560 | tf_op jit(solution)/shard_map/dot_general | solution.py:23
  198.1 35.5 %shard_map.81 = (bf16[512,1856]{1,0:T(8,128)(2,1)}, bf16[512,1856]{1,0:T(8,128)(2,1)}) custom-call(bf16[512,1856]{1,0:T(8,128)(2,1)} %convolution_convert_fusion.1.refs_0_, bf16[64,1856]{1,0:T(8,128)(2,1)} %multiply_convert_fusion.refs_1_), custom_call_target="tpu_custom_call" | custom-call | tf_op jit(solution)/shard_map/pallas_call | solution.py:365
  233.7 6.1 %convolution_convert_fusion.7.refs_1_ = bf16[512,1024]{1,0:T(8,128)(2,1)} fusion(bf16[512,1856]{1,0:T(8,128)(2,1)} %get-tuple-element.21, bf16[1024,1856]{0,1:T(8,128)(2,1)} %param.8), kind=kOutput, calls=%fused_computation.18 | convolution fusion | flops 1946681344 | bytes 6750208 | tf_op jit(solution)/shard_map/dot_general | solution.py:23
  239.8 5.7 %convolution_convert_fusion.refs_0_ = bf16[512,1856]{1,0:T(8,128)(2,1)} fusion(bf16[512,1856]{1,0:T(8,128)(2,1)S(1)} %copy-done.6, bf16[1856,1856]{1,0:T(8,128)(2,1)S(1)} %bitcast.22), kind=kOutput, calls=%fused_computation.7 | convolution fusion | flops 3528359936 | bytes 10690560 | tf_op jit(solution)/shard_map/dot_general | solution.py:23
  245.5 41.6 %shard_map.82 = (bf16[512,1856]{1,0:T(8,128)(2,1)}, bf16[512,1024]{1,0:T(8,128)(2,1)}) custom-call(bf16[512,1856]{1,0:T(8,128)(2,1)} %convolution_convert_fusion.refs_0_, bf16[512,1024]{1,0:T(8,128)(2,1)} %convolution_convert_fusion.7.refs_1_), custom_call_target="tpu_custom_call" | custom-call | tf_op jit(solution)/shard_map/pallas_call | solution.py:365
  287.2 6.1 %convolution_convert_fusion.6.refs_0_ = bf16[512,1024]{1,0:T(8,128)(2,1)} fusion(bf16[512,1856]{1,0:T(8,128)(2,1)} %get-tuple-element.23, bf16[1024,1856]{0,1:T(8,128)(2,1)} %param.8), kind=kOutput, calls=%fused_computation.17 | convolution fusion | flops 1946681344 | bytes 6750208 | tf_op jit(solution)/shard_map/dot_general | solution.py:23
  293.2 36.1 %shard_map.83 = bf16[512,1024]{1,0:T(8,128)(2,1)} custom-call(bf16[512,1024]{1,0:T(8,128)(2,1)} %convolution_convert_fusion.6.refs_0_), custom_call_target="tpu_custom_call" | custom-call | tf_op jit(solution)/shard_map/pallas_call | solution.py:365
  329.4 3.1 fusion.7
  332.4 12.8 %fusion = f32[1856,1856]{1,0:T(8,128)} fusion(bf16[512,1856]{1,0:T(8,128)(2,1)S(1)} %copy-done.4, bf16[512,1856]{1,0:T(8,128)(2,1)S(1)} %copy-done.3, bf16[512,1856]{1,0:T(8,128)(2,1)} %get-tuple-element.20, bf16[512,1856]{1,0:T(8,128)(2,1)S(1)} %copy-done.5), kind=kOutput, calls=%fused_computation | convolution fusion | flops 7070023680 | bytes 21381120 | tf_op jit(solution)/shard_map/dot_general | solution.py:27
  (24 shorter events, 0.2 us)
Async XLA Ops:
  0.6 4.5 %copy-start = (bf16[128,2048]{1,0:T(8,128)(2,1)S(1)}, bf16[128,2048]{1,0:T(8,128)(2,1)}, u32[]{:S(2)}) copy-start(bf16[128,2048]{1,0:T(8,128)(2,1)} %refs_2_.1) | copy-start | bytes 1572868
  0.6 3.9 %copy-start.1 = (bf16[128,1856]{0,1:T(8,128)(2,1)S(1)}, bf16[128,1856]{0,1:T(8,128)(2,1)}, u32[]{:S(2)}) copy-start(bf16[128,1856]{0,1:T(8,128)(2,1)} %param.11) | copy-start | bytes 1425412
  75.0 6.2 %copy-start.2 = (bf16[512,1856]{1,0:T(8,128)(2,1)S(1)}, bf16[512,1856]{1,0:T(8,128)(2,1)}, u32[]{:S(2)}) copy-start(bf16[512,1856]{1,0:T(8,128)(2,1)} %get-tuple-element.15) | copy-start | bytes 5701636
  198.1 41.7 %slice-start = ((s8[7127040]{0:T(1024)(128)(4,1)}), s8[2932736]{0:T(1024)(128)(4,1)S(1)}, s32[]{:S(2)}) async-start(s8[7127040]{0:T(1024)(128)(4,1)} %bitcast.21), calls=%async_computation | async-start | bytes 5865472
  233.7 6.1 %slice-start.1 = ((s8[7127040]{0:T(1024)(128)(4,1)}), s8[4194304]{0:T(1024)(128)(4,1)S(1)}, s32[]{:S(2)}) async-start(s8[7127040]{0:T(1024)(128)(4,1)} %bitcast.21), calls=%async_computation.1 | async-start | bytes 8388608
  233.7 6.1 %copy-start.6 = (bf16[512,1856]{1,0:T(8,128)(2,1)S(1)}, bf16[512,1856]{1,0:T(8,128)(2,1)}, u32[]{:S(2)}) copy-start(bf16[512,1856]{1,0:T(8,128)(2,1)} %get-tuple-element.20) | copy-start | bytes 5701636
  287.1 42.2 %copy-start.7 = (bf16[512,1024]{1,0:T(8,128)(2,1)S(1)}, bf16[512,1024]{1,0:T(8,128)(2,1)}, u32[]{:S(2)}) copy-start(bf16[512,1024]{1,0:T(8,128)(2,1)} %get-tuple-element.22) | copy-start | bytes 3145732
  287.1 42.2 %copy-start.8 = (bf16[1024,256]{1,0:T(8,128)(2,1)S(1)}, bf16[1024,256]{1,0:T(8,128)(2,1)}, u32[]{:S(2)}) copy-start(bf16[1024,256]{1,0:T(8,128)(2,1)} %get-tuple-element.13) | copy-start | bytes 1572868
  293.2 39.2 %copy-start.3 = (bf16[512,1856]{1,0:T(8,128)(2,1)S(1)}, bf16[512,1856]{1,0:T(8,128)(2,1)}, u32[]{:S(2)}) copy-start(bf16[512,1856]{1,0:T(8,128)(2,1)} %get-tuple-element.15) | copy-start | bytes 5701636
  329.3 3.1 copy-start.4
  329.4 3.1 copy-start.5
